TPU v7x, 256 devices: a whole 4x4x8 slice. The times are simulated.
256 devices in a mesh: role: 2 (over core), dp: 32 (over x, z), mp: 4 (over y).
Axes of the slice: x: 4, y: 4, z: 8, core: 2. Of those that a mesh axis runs over, the one named last changes fastest.
Arguments:
- noise: bfloat16 [4096, 3072], P('dp', 'mp'), may hold values from -6 to 6
- gen_gain: float32 [3072], replicated, may hold values from 0.25 to 1.75
- gen_weight: bfloat16 [3072, 3072], P('dp', 'mp'), may hold values from -0.109375 to 0.109375
- routes: int32 [1024, 1], replicated, may hold values from 0 to 31; in each aligned block of 32 rows (0 to 31, 32 to 63, ...) at most 2 rows name the same one
- critic_noise: bfloat16 [8192, 3072], P('dp', 'mp'), may hold values from -6 to 6
- critic_steps: int32 [2048], P('dp'), may hold values from 20 to 979
- crit_mod: float32 [2, 2, 3072], P('role'), may hold values from -3 to 3
- crit_first: bfloat16 [2, 3072, 3072], P('role', 'dp', 'mp'), may hold values from -0.109375 to 0.109375
- crit_second: bfloat16 [2, 3072, 3072], P('role', 'dp', 'mp'), may hold values from -0.109375 to 0.109375
Outputs:
- noise_grad: float32 [4096, 4, 2, 384], P('dp', 'mp', 'role')
- grad_first: float32 [2, 3072, 3072], P('role', 'dp', 'mp')
- grad_second: float32 [2, 3072, 3072], P('role', 'dp', 'mp')
Inputs may be any that keep to these rules, and one draw needn't show every extreme that they name: `routes`: within the 32 rows of one index of dp, no value appears more than 2 times, and in every draw some value appears exactly 2 times in some such block.
All inputs are finite; a program needn't handle non-finite values.
Results may differ from a plain program's by a relative error of at most 0.01.
Values may be sent and summed in bfloat16 or wider, within the bound.
A program may use at most 128 MiB of HBM per device.

v0:
```python
import jax
import jax.numpy as jnp
from jax import lax
from jax.sharding import Mesh
from jax.sharding import PartitionSpec as P

D = 3072
TOK_DEV = 128
BT = 4
DP = ("dp_0", "dp_1")
epsilon = 1e-06
levels = 1000.0


def copy_for_each(shard, axis):
    length = lax.axis_size(axis)
    return lax.all_to_all(
        jnp.broadcast_to(shard[None], (length, *shard.shape)), axis, 0, 0, tiled=True
    )


def joined_along(pieces, dim):
    pieces = jnp.moveaxis(pieces, 0, dim)
    shape = pieces.shape
    return pieces.reshape(*shape[:dim], shape[dim] * shape[dim + 1], *shape[dim + 2 :])


def collect(shard, axis, dim):
    pieces = copy_for_each(shard, axis)
    return joined_along(pieces, dim)


def summed_rows(shard, axes, dim):
    for axis in axes:
        shard = lax.psum_scatter(shard, axis, scatter_dimension=dim, tiled=True)
    return shard


def cut_along(shard, dim, length):
    before, after = (shard.shape[:dim], shard.shape[dim + 1 :])
    return jnp.moveaxis(shard.reshape(*before, length, -1, *after), dim, 0)


def summed_on_arrival(shard, axis, dim):
    length = lax.axis_size(axis)
    pieces = lax.all_to_all(cut_along(shard, dim, length), axis, 0, 0, tiled=True)
    return jnp.sum(pieces.astype(jnp.float32), axis=0)


def of_everyone(shard, axis):
    return copy_for_each(shard, axis).sum(axis=0)


def from_partner(block, axis, apart):
    count = lax.axis_size(axis)
    route = []
    for low in range(count):
        high = low | 1 << apart
        if high != low and high < count:
            route += [(low, high), (high, low)]
    return lax.ppermute(block, axis, route)


def norm_act(field, scale):
    root = lax.rsqrt(jnp.mean(field * field, axis=-1, keepdims=True) + epsilon)
    normed = field * root
    shaped = normed * scale
    return (jax.nn.silu(shaped).astype(jnp.bfloat16), normed, shaped, root)


def slope(shaped):
    sigma = jax.nn.sigmoid(shaped)
    return sigma * (1.0 + shaped * (1.0 - sigma))


def widen(field):
    return collect(field, "mp", 1)


def layer_rows(weight):
    return lax.all_gather(weight, DP, axis=0, tiled=True)


def weight_sum(left, right):
    term = lax.dot_general(
        left, right, (((0,), (0,)), ((), ())), preferred_element_type=jnp.float32
    )
    return summed_rows(term.astype(jnp.bfloat16), DP, 0).astype(jnp.float32)


def row_back(delta, weight, normed, shaped, root, scale):
    width = weight.shape[1]
    offset = lax.axis_index("mp") * width
    partial_rows = lax.dot_general(
        delta, weight, (((1,), (1,)), ((), ())), preferred_element_type=jnp.float32
    )
    owned = summed_on_arrival(partial_rows.astype(jnp.bfloat16), "mp", 1)
    normed_mine = lax.dynamic_slice_in_dim(normed, offset, width, 1)
    shaped_mine = lax.dynamic_slice_in_dim(shaped, offset, width, 1)
    scale_mine = lax.dynamic_slice_in_dim(jnp.broadcast_to(scale, normed.shape), offset, width, 1)
    grad_norm = owned * slope(shaped_mine) * scale_mine
    inner = of_everyone(jnp.sum(grad_norm * normed_mine, axis=-1), "mp")
    return root * (grad_norm - normed_mine * (inner[:, None] / D))


def shards(
    noise,
    gen_gain,
    gen_weight,
    routes,
    critic_noise,
    critic_steps,
    crit_mod,
    crit_first,
    crit_second,
):
    width = noise.shape[1]
    groups = lax.axis_size(DP)
    me_index = lax.axis_index(DP)
    blocks_here = noise.shape[0] // BT
    most = 2 * blocks_here // groups
    noise_f = noise.astype(jnp.float32)
    gen_scale = gen_gain[None, :]
    gen_act, gen_normed, gen_shaped, gen_root = norm_act(
        widen(noise).astype(jnp.float32), gen_scale
    )
    gen_full = layer_rows(gen_weight)
    generated = (noise_f + jnp.dot(gen_act, gen_full, preferred_element_type=jnp.float32)).astype(
        jnp.bfloat16
    )
    table = routes[:, 0]
    target_index = lax.dynamic_slice_in_dim(table, me_index * blocks_here, blocks_here, 0)
    order = jnp.arange(blocks_here, dtype=jnp.int32)
    earlier = (target_index[:, None] == target_index[None, :]) & (order[None, :] < order[:, None])
    rank = jnp.sum(earlier.astype(jnp.int32), axis=1)
    slot_here = target_index * most + rank
    placing = (jnp.arange(groups * most, dtype=jnp.int32)[:, None] == slot_here[None, :]).astype(
        jnp.bfloat16
    )
    outgoing = jnp.dot(
        placing, generated.reshape(blocks_here, BT * width), preferred_element_type=jnp.float32
    )
    outgoing = outgoing.astype(jnp.bfloat16).reshape(groups, most * BT, width)
    incoming = lax.all_to_all(outgoing, DP, split_axis=0, concat_axis=0, tiled=True)
    clean = incoming.reshape(groups * most * BT, width)
    counts = jnp.sum((table.reshape(groups, blocks_here) == me_index).astype(jnp.int32), axis=1)
    filled = (jnp.arange(most, dtype=jnp.int32)[None, :] < counts[:, None]).astype(jnp.float32)
    valid = jnp.repeat(filled.reshape(groups * most), BT)[:, None]
    level = jnp.repeat(critic_steps.astype(jnp.float32) / levels, BT)[:, None]
    clean_f = clean.astype(jnp.float32)
    crit_noise_f = critic_noise.astype(jnp.float32)
    noisy = ((1.0 - level) * clean_f + level * crit_noise_f).astype(jnp.bfloat16)
    target = crit_noise_f - clean_f
    modulation = crit_mod[0]
    scale_one = 1.0 + level * modulation[0][None, :]
    scale_two = 1.0 + level * modulation[1][None, :]
    first, _, _, _ = norm_act(widen(noisy).astype(jnp.float32), scale_one)
    first_full = layer_rows(crit_first[0])
    first_out = jnp.dot(first, first_full, preferred_element_type=jnp.float32)
    hidden = (noisy.astype(jnp.float32) + first_out).astype(jnp.bfloat16)
    second, normed, shaped, root = norm_act(widen(hidden).astype(jnp.float32), scale_two)
    second_full = layer_rows(crit_second[0])
    pred = (
        hidden.astype(jnp.float32)
        + jnp.dot(second, second_full, preferred_element_type=jnp.float32)
    ).astype(jnp.bfloat16)
    delta = ((pred.astype(jnp.float32) - target) * valid / TOK_DEV).astype(jnp.bfloat16)
    grad_two = weight_sum(second, delta)
    upstream = (
        delta.astype(jnp.float32) + row_back(delta, second_full, normed, shaped, root, scale_two)
    ).astype(jnp.bfloat16)
    grad_one = weight_sum(first, upstream)
    other = from_partner(pred, "role", 0)
    pred_f = pred.astype(jnp.float32)
    other_f = other.astype(jnp.float32)
    difference = jnp.where(lax.axis_index("role") == 1, pred_f - other_f, other_f - pred_f)
    gap = ((1.0 - level) * difference).astype(jnp.bfloat16).reshape(groups, most * BT, width)
    coming_back = lax.all_to_all(gap, DP, split_axis=0, concat_axis=0, tiled=True)
    back_slots = coming_back.reshape(groups * most, BT * width)
    picked = lax.dot_general(
        placing, back_slots, (((0,), (0,)), ((), ())), preferred_element_type=jnp.float32
    )
    returned = picked.astype(jnp.bfloat16).reshape(blocks_here * BT, width)
    noise_grad = returned.astype(jnp.float32) + row_back(
        returned, gen_full, gen_normed, gen_shaped, gen_root, gen_scale
    )
    half_width = width // 2
    my_half = lax.dynamic_slice_in_dim(
        noise_grad, lax.axis_index("role") * half_width, half_width, 1
    )
    return (my_half.reshape(noise_grad.shape[0], 1, 1, half_width), grad_one[None], grad_two[None])


def solution(mesh):
    split = Mesh(
        mesh.devices.reshape(mesh.shape["role"], 4, 8, mesh.shape["mp"]),
        ("role", "dp_0", "dp_1", "mp"),
    )
    in_specs = (
        P(DP, "mp"),
        P(),
        P(DP, "mp"),
        P(),
        P(DP, "mp"),
        P(DP),
        P("role", None, None),
        P("role", DP, "mp"),
        P("role", DP, "mp"),
    )
    out_specs = (P(DP, "mp", "role", None), P("role", DP, "mp"), P("role", DP, "mp"))
    return jax.shard_map(
        shards, mesh=split, in_specs=in_specs, out_specs=out_specs, check_vma=False
    )
```

profile of v0, /device:TPU:2, one launch (start us, length us, event | category | flops | bytes accessed | tf_op | source)
XLA Modules:
  0.0 479.6 jit_solution(8404089671905882432)
XLA Ops:
  8.6 1.9 broadcast_in_dim.25
  10.6 4.5 all-to-all-start
  17.4 9.9 %all-to-all-done = bf16[4,128,768]{2,1,0:T(8,128)(2,1)S(1)} async-done(((bf16[4,128,768]{2,1,0:T(8,128)(2,1)}), bf16[4,128,768]{2,1,0:T(8,128)(2,1)S(1)}, u32[]{:S(2)}, u32[]{:S(2)}) %all-to-all-start) | async-done | bytes 786464 | tf_op jit(solution)/shard_map/all_to_all | solution.py:17
  27.8 1.7 copy.45
  29.9 3.0 broadcast_multiply_fusion.1
  32.9 62.3 %all-gather.6.cloned.1.call-done = bf16[3072,768]{1,0:T(8,128)(2,1)} async-done(((bf16[96,768]{1,0:T(8,128)(2,1)}), bf16[3072,768]{1,0:T(8,128)(2,1)}) %all-gather.6.cloned.1.call-update) | async-done | bytes 4718608 | tf_op jit(solution)/shard_map/all_gather | solution.py:81
  95.2 3.4 fusion.23
  99.0 1.0 reshape.127
  100.0 7.2 %all-to-all-start.1 = ((bf16[32,8,768]{2,1,0:T(8,128)(2,1)}), bf16[32,8,768]{2,1,0:T(8,128)(2,1)S(1)}, u32[]{:S(2)}, u32[]{:S(2)}) async-start(bf16[32,8,768]{2,1,0:T(8,128)(2,1)} %reshape.127), calls=%async_computation.1 | async-start | bytes 786432 | tf_op jit(solution)/shard_map/all_to_all | solution.py:144
  107.5 11.1 %all-to-all-done.1 = bf16[32,8,768]{2,1,0:T(8,128)(2,1)S(1)} async-done(((bf16[32,8,768]{2,1,0:T(8,128)(2,1)}), bf16[32,8,768]{2,1,0:T(8,128)(2,1)S(1)}, u32[]{:S(2)}, u32[]{:S(2)}) %all-to-all-start.1) | async-done | bytes 393248 | tf_op jit(solution)/shard_map/all_to_all | solution.py:144
  118.8 1.3 broadcast_in_dim.26
  120.1 4.3 all-to-all-start.2
  124.4 14.9 %all-to-all-done.2 = bf16[4,256,768]{2,1,0:T(8,128)(2,1)S(1)} async-done(((bf16[4,256,768]{2,1,0:T(8,128)(2,1)}), bf16[4,256,768]{2,1,0:T(8,128)(2,1)S(1)}, u32[]{:S(2)}, u32[]{:S(2)}) %all-to-all-start.2) | async-done | bytes 1572896 | tf_op jit(solution)/shard_map/all_to_all | solution.py:17
  139.6 2.1 copy.56
  142.0 36.2 %all-gather.8.cloned.1.call-done = bf16[1,3072,768]{2,1,0:T(8,128)(2,1)} async-done(((bf16[1,96,768]{2,1,0:T(8,128)(2,1)}), bf16[1,3072,768]{2,1,0:T(8,128)(2,1)}) %all-gather.8.cloned.1.call-update) | async-done | bytes 4718608 | tf_op jit(solution)/shard_map/all_gather | solution.py:81
  178.2 5.3 %fusion.20 = bf16[256,768]{1,0:T(8,128)(2,1)S(1)} fusion(bf16[1,3072,768]{2,1,0:T(8,128)(2,1)} %all-gather.8.cloned.1.call-done, bf16[256,768]{1,0:T(8,128)(2,1)S(1)} %fusion.26, f32[256,3072]{1,0:T(8,128)} %bitcast.73, f32[3072]{0:T(1024)S(1)} %bitcast.78, f32[256]{0:T(256)S(1)} %broadcast_in_dim_reshape.4, f32[256]{0:T(256)S(1)} %add_rsqrt_fusion.1), kind=kOutput, calls=%fused_computation.30 | convolution fusion | flops 1215627264 | bytes 8665088 | tf_op jit(solution)/shard_map/dot_general | solution.py:159
  183.6 21.2 %all_to_all.47 = bf16[4,256,768]{2,1,0:T(8,128)(2,1)S(1)} all-to-all(bf16[4,256,768]{2,1,0:T(8,128)(2,1)S(1)} %broadcast_in_dim.27), channel_id=1, replica_groups=mesh['role'=2,'dp_0'=4,'dp_1'=8,'mp'=4] {'mp'}, dimensions={0} | all-to-all | bytes 3145728 | tf_op jit(solution)/shard_map/all_to_all | solution.py:17
  206.4 3.8 fusion.24
  210.2 50.7 %all-gather.10.cloned.1.call-done = bf16[1,3072,768]{2,1,0:T(8,128)(2,1)} async-done(((bf16[1,96,768]{2,1,0:T(8,128)(2,1)}), bf16[1,3072,768]{2,1,0:T(8,128)(2,1)}) %all-gather.10.cloned.1.call-update) | async-done | bytes 4718608 | tf_op jit(solution)/shard_map/all_gather | solution.py:81
  260.9 5.0 %fusion.17 = bf16[256,768]{1,0:T(8,128)(2,1)} fusion(bf16[1,3072,768]{2,1,0:T(8,128)(2,1)} %all-gather.10.cloned.1.call-done, bf16[256,768]{1,0:T(8,128)(2,1)} %copy-done.6, f32[256,3072]{1,0:T(8,128)S(1)} %get-tuple-element.19), kind=kOutput, calls=%fused_computation.29 | convolution fusion | flops 1212481536 | bytes 8650752 | tf_op jit(solution)/shard_map/dot_general | solution.py:165
  269.3 1.4 broadcast_in_dim.29
  270.7 0.9 mul.255
  271.6 2.3 fusion.32
  274.7 4.3 convolution_convert_fusion
  279.0 1.0 copy-done.5
  280.0 3.8 fusion.6
  283.7 1.3 copy.60
  285.1 4.3 all-to-all-start.7
  289.4 21.4 %all-to-all-done.7 = bf16[4,256,768]{2,1,0:T(8,128)(2,1)S(1)} async-done(((bf16[4,256,768]{2,1,0:T(8,128)(2,1)}), bf16[4,256,768]{2,1,0:T(8,128)(2,1)S(1)}, u32[]{:S(2)}, u32[]{:S(2)}) %all-to-all-start.7) | async-done | bytes 1572896 | tf_op jit(solution)/shard_map/all_to_all | solution.py:46
  311.0 3.1 multiply_reduce_fusion.1
  314.1 7.6 %all_to_all.48 = f32[4,1,256]{2,1,0:T(1,128)S(1)} all-to-all(f32[4,1,256]{2,1,0:T(1,128)S(1)} %broadcast_in_dim.30), channel_id=1, replica_groups=mesh['role'=2,'dp_0'=4,'dp_1'=8,'mp'=4] {'mp'}, dimensions={0} | all-to-all | bytes 8192 | tf_op jit(solution)/shard_map/all_to_all | solution.py:17
  321.8 6.0 %convolution_convert_fusion.1 = bf16[3072,768]{1,0:T(8,128)(2,1)} fusion(f32[256,768]{1,0:T(8,128)} %get-tuple-element.16, bf16[256,768]{1,0:T(8,128)(2,1)S(1)} %copy-done.5, f32[256,3072]{1,0:T(8,128)} %get-tuple-element.20, s32[]{:T(128)S(6)} %select_n.25, f32[256]{0:T(256)S(1)} %broadcast_multiply_fusion.3, f32[256]{0:T(256)S(1)} %copy-done.18, ...), kind=kOutput, calls=%fused_computation.1 | convolution fusion | flops 1218576384 | bytes 9846788 | tf_op jit(solution)/shard_map/dot_general | solution.py:85
  327.9 2.2 reduce-scatter.9.cloned.1.call-done
  330.2 9.9 %all-to-all-start.4 = ((bf16[32,8,768]{2,1,0:T(8,128)(2,1)}), bf16[32,8,768]{2,1,0:T(8,128)(2,1)S(1)}, u32[]{:S(2)}, u32[]{:S(2)}) async-start(bf16[32,8,768]{2,1,0:T(8,128)(2,1)} %get-tuple-element.24), calls=%async_computation.4 | async-start | bytes 786432 | tf_op jit(solution)/shard_map/all_to_all | solution.py:178
  340.1 48.6 %reduce-scatter.5.cloned.1.call-done = bf16[768,768]{1,0:T(8,128)(2,1)} async-done(((bf16[3072,768]{1,0:T(8,128)(2,1)}), bf16[768,768]{1,0:T(8,128)(2,1)}) %reduce-scatter.5.cloned.1.call-update) | async-done | bytes 1179664 | tf_op jit(solution)/shard_map/reduce_scatter | solution.py:35
  389.4 4.0 convolution_convert_fusion.2
  393.3 0.9 copy.61
  394.3 4.3 all-to-all-start.5
  399.4 11.5 %all-to-all-done.5 = bf16[4,128,768]{2,1,0:T(8,128)(2,1)S(1)} async-done(((bf16[4,128,768]{2,1,0:T(8,128)(2,1)}), bf16[4,128,768]{2,1,0:T(8,128)(2,1)S(1)}, u32[]{:S(2)}, u32[]{:S(2)}) %all-to-all-start.5) | async-done | bytes 786464 | tf_op jit(solution)/shard_map/all_to_all | solution.py:46
  411.0 1.4 multiply_reduce_fusion.2
  412.9 3.2 all-to-all-start.6
  416.2 5.2 %all-to-all-done.6 = f32[4,1,128]{2,1,0:T(1,128)S(1)} async-done(((f32[4,1,128]{2,1,0:T(1,128)}), f32[4,1,128]{2,1,0:T(1,128)S(1)}, u32[]{:S(2)}, u32[]{:S(2)}) %all-to-all-start.6) | async-done | bytes 2080 | tf_op jit(solution)/shard_map/all_to_all | solution.py:17
  421.4 1.0 fusion.39
  422.4 0.9 copy.52
  423.3 7.0 %reduce-scatter.11.cloned.1.call-done = bf16[96,768]{1,0:T(8,128)(2,1)} async-done(((bf16[768,768]{1,0:T(8,128)(2,1)}), bf16[96,768]{1,0:T(8,128)(2,1)}) %reduce-scatter.11.cloned.1.call-update) | async-done | bytes 147472 | tf_op jit(solution)/shard_map/reduce_scatter | solution.py:35
  430.3 1.6 bitcast_convert_fusion
  431.9 39.2 %reduce-scatter.7.cloned.1.call-done = bf16[96,768]{1,0:T(8,128)(2,1)} async-done(((bf16[768,768]{1,0:T(8,128)(2,1)}), bf16[96,768]{1,0:T(8,128)(2,1)}) %reduce-scatter.7.cloned.1.call-update) | async-done | bytes 147472 | tf_op jit(solution)/shard_map/reduce_scatter | solution.py:35
  471.1 1.6 bitcast_convert_fusion.1
  (102 shorter events, 14.6 us)
Async XLA Ops:
  7.2 88.1 %all-gather.6.cloned.1.call-start = ((), (), s32[]{:S(2)}) async-start(), calls=%async_computation.13 | async-start | bytes 4866048 | tf_op jit(solution)/shard_map/all_gather | solution.py:81
  7.9 170.3 %all-gather.8.cloned.1.call-start = ((), (), s32[]{:S(2)}) async-start(), calls=%async_computation.18 | async-start | bytes 4866048 | tf_op jit(solution)/shard_map/all_gather | solution.py:81
  10.6 16.7 %all-to-all-start = ((bf16[4,128,768]{2,1,0:T(8,128)(2,1)}), bf16[4,128,768]{2,1,0:T(8,128)(2,1)S(1)}, u32[]{:S(2)}, u32[]{:S(2)}) async-start(bf16[4,128,768]{2,1,0:T(8,128)(2,1)} %broadcast_in_dim.25), calls=%async_computation | async-start | bytes 1572864 | tf_op jit(solution)/shard_map/all_to_all | solution.py:17
  15.0 245.9 %all-gather.10.cloned.1.call-start = ((), (), s32[]{:S(2)}) async-start(), calls=%async_computation.19 | async-start | bytes 4866048 | tf_op jit(solution)/shard_map/all_gather | solution.py:81
  17.4 81.4 %copy-start.15 = (s32[32]{0:T(128)}, s32[32]{0:T(128)S(1)}, u32[]{:S(2)}) copy-start(s32[32]{0:T(128)S(1)} %multiply_add_fusion.1) | copy-start | bytes 388
  27.7 2.2 copy-start.9
  29.5 65.8 %copy-start.7 = (bf16[128,768]{1,0:T(8,128)(2,1)S(1)}, bf16[128,768]{1,0:T(8,128)(2,1)}, u32[]{:S(2)}) copy-start(bf16[128,768]{1,0:T(8,128)(2,1)} %param.9) | copy-start | bytes 589828
  29.9 65.3 %copy-start.19 = (f32[128]{0:T(128)}, f32[128]{0:T(128)S(1)}, u32[]{:S(2)}) copy-start(f32[128]{0:T(128)S(1)} %add_rsqrt_fusion.2) | copy-start | bytes 1540
  32.9 65.7 %copy-start.2 = (f32[128,3072]{1,0:T(8,128)}, f32[128,3072]{1,0:T(8,128)S(1)}, u32[]{:S(2)}) copy-start(f32[128,3072]{1,0:T(8,128)S(1)} %get-tuple-element.21) | copy-start | bytes 4718596
  95.2 12.1 %copy-start.22 = (s32[64]{0:T(128)S(1)}, s32[64]{0:T(128)}, u32[]{:S(2)}) copy-start(s32[64]{0:T(128)} %param.14) | copy-start | bytes 772
  95.2 23.4 %copy-start.3 = (bf16[256,768]{1,0:T(8,128)(2,1)S(1)}, bf16[256,768]{1,0:T(8,128)(2,1)}, u32[]{:S(2)}) copy-start(bf16[256,768]{1,0:T(8,128)(2,1)} %param.13) | copy-start | bytes 1179652
  100.0 18.6 %all-to-all-start.1 = ((bf16[32,8,768]{2,1,0:T(8,128)(2,1)}), bf16[32,8,768]{2,1,0:T(8,128)(2,1)S(1)}, u32[]{:S(2)}, u32[]{:S(2)}) async-start(bf16[32,8,768]{2,1,0:T(8,128)(2,1)} %reshape.127), calls=%async_computation.1 | async-start | bytes 786432 | tf_op jit(solution)/shard_map/all_to_all | solution.py:144
  107.5 98.3 %copy-start.10 = (f32[256]{0:T(256)}, f32[256]{0:T(256)S(1)}, u32[]{:S(2)}) copy-start(f32[256]{0:T(256)S(1)} %broadcast_in_dim_reshape.4) | copy-start | bytes 3076
  107.5 12.6 %copy-start.13 = (f32[256]{0:T(256)}, f32[256]{0:T(256)S(1)}, u32[]{:S(2)}) copy-start(f32[256]{0:T(256)S(1)} %broadcast_subtract_fusion) | copy-start | bytes 3076
  107.5 16.9 %copy-start.8 = (f32[1,2,3072]{2,1,0:T(2,128)S(1)}, f32[1,2,3072]{2,1,0:T(2,128)}, u32[]{:S(2)}) copy-start(f32[1,2,3072]{2,1,0:T(2,128)} %param.15) | copy-start | bytes 73732
  120.1 19.2 %all-to-all-start.2 = ((bf16[4,256,768]{2,1,0:T(8,128)(2,1)}), bf16[4,256,768]{2,1,0:T(8,128)(2,1)S(1)}, u32[]{:S(2)}, u32[]{:S(2)}) async-start(bf16[4,256,768]{2,1,0:T(8,128)(2,1)} %broadcast_in_dim.26), calls=%async_computation.2 | async-start | bytes 3145728 | tf_op jit(solution)/shard_map/all_to_all | solution.py:17
  124.4 205.8 %reduce-scatter.9.cloned.1.call-start = ((), (), s32[]{:S(2)}) async-start(), calls=%async_computation.16 | async-start | bytes 5898240 | tf_op jit(solution)/shard_map/reduce_scatter | solution.py:35
  124.4 53.8 %copy-start.12 = (f32[1,1,3072]{2,1,0:T(1,128)}, f32[1,1,3072]{2,1,0:T(1,128)S(1)}, u32[]{:S(2)}) copy-start(f32[1,1,3072]{2,1,0:T(1,128)S(1)} %get-tuple-element.26) | copy-start | bytes 36868
  142.0 41.5 %copy-start.21 = (f32[256]{0:T(256)}, f32[256]{0:T(256)S(1)}, u32[]{:S(2)}) copy-start(f32[256]{0:T(256)S(1)} %add_rsqrt_fusion.1) | copy-start | bytes 3076
  183.5 21.5 %copy-start.6 = (bf16[256,768]{1,0:T(8,128)(2,1)}, bf16[256,768]{1,0:T(8,128)(2,1)S(1)}, u32[]{:S(2)}) copy-start(bf16[256,768]{1,0:T(8,128)(2,1)S(1)} %fusion.20) | copy-start | bytes 1179652
  205.8 0.6 copy-start.17
  210.2 63.7 %copy-start = (f32[256,3072]{1,0:T(8,128)}, f32[256,3072]{1,0:T(8,128)S(1)}, u32[]{:S(2)}) copy-start(f32[256,3072]{1,0:T(8,128)S(1)} %get-tuple-element.19) | copy-start | bytes 9437188
  260.9 5.0 %copy-start.14 = (s32[1024,1]{0,1:T(1,128)S(1)}, s32[1024,1]{0,1:T(1,128)}, u32[]{:S(2)}) copy-start(s32[1024,1]{0,1:T(1,128)} %param.12) | copy-start | bytes 12292
  265.9 5.7 %collective-permute-start = (bf16[256,768]{1,0:T(8,128)(2,1)}, bf16[256,768]{1,0:T(8,128)(2,1)}, u32[]{:S(2)}, u32[]{:S(2)}) collective-permute-start(bf16[256,768]{1,0:T(8,128)(2,1)} %fusion.17), channel_id=1, source_target_pairs={{0,128},{128,0},{1,129},{129,1},{2,130},{130,2},{3,131},{131,3},{4... | collective-permute-start | bytes 1179656 | tf_op jit(solution)/shard_map/ppermute | solution.py:61
  273.9 0.8 copy-start.4
  279.0 1.0 copy-start.5
  285.1 25.7 %all-to-all-start.7 = ((bf16[4,256,768]{2,1,0:T(8,128)(2,1)}), bf16[4,256,768]{2,1,0:T(8,128)(2,1)S(1)}, u32[]{:S(2)}, u32[]{:S(2)}) async-start(bf16[4,256,768]{2,1,0:T(8,128)(2,1)} %bitcast.68), calls=%async_computation.7 | async-start | bytes 3145728 | tf_op jit(solution)/shard_map/all_to_all | solution.py:46
  289.4 99.3 %reduce-scatter.5.cloned.1.call-start = ((), (), s32[]{:S(2)}) async-start(), calls=%async_computation.14 | async-start | bytes 5898240 | tf_op jit(solution)/shard_map/reduce_scatter | solution.py:35
  289.4 32.4 %copy-start.11 = (f32[256]{0:T(256)S(1)}, f32[256]{0:T(256)}, u32[]{:S(2)}) copy-start(f32[256]{0:T(256)} %copy-done.10) | copy-start | bytes 3076
  289.4 32.4 %copy-start.18 = (f32[256]{0:T(256)S(1)}, f32[256]{0:T(256)}, u32[]{:S(2)}) copy-start(f32[256]{0:T(256)} %copy-done.17) | copy-start | bytes 3076
  311.0 10.8 %copy-start.1 = (f32[4,32,8,768]{3,2,0,1:T(8,128)S(1)}, f32[4,32,8,768]{3,2,0,1:T(8,128)}, u32[]{:S(2)}) copy-start(f32[4,32,8,768]{3,2,0,1:T(8,128)} %copy.56) | copy-start | bytes 9437188
  327.8 61.1 %copy-start.16 = (s32[32]{0:T(128)S(1)}, s32[32]{0:T(128)}, u32[]{:S(2)}) copy-start(s32[32]{0:T(128)} %copy-done.15) | copy-start | bytes 388
  327.9 102.4 %reduce-scatter.11.cloned.1.call-start = ((), (), s32[]{:S(2)}) async-start(), calls=%async_computation.17 | async-start | bytes 1327104 | tf_op jit(solution)/shard_map/reduce_scatter | solution.py:35
  330.2 58.5 %all-to-all-start.4 = ((bf16[32,8,768]{2,1,0:T(8,128)(2,1)}), bf16[32,8,768]{2,1,0:T(8,128)(2,1)S(1)}, u32[]{:S(2)}, u32[]{:S(2)}) async-start(bf16[32,8,768]{2,1,0:T(8,128)(2,1)} %get-tuple-element.24), calls=%async_computation.4 | async-start | bytes 786432 | tf_op jit(solution)/shard_map/all_to_all | solution.py:178
  340.0 131.1 %reduce-scatter.7.cloned.1.call-start = ((), (), s32[]{:S(2)}) async-start(), calls=%async_computation.15 | async-start | bytes 1327104 | tf_op jit(solution)/shard_map/reduce_scatter | solution.py:35
  393.3 28.0 %copy-start.20 = (f32[128]{0:T(128)S(1)}, f32[128]{0:T(128)}, u32[]{:S(2)}) copy-start(f32[128]{0:T(128)} %copy-done.19) | copy-start | bytes 1540
  394.3 16.6 %all-to-all-start.5 = ((bf16[4,128,768]{2,1,0:T(8,128)(2,1)}), bf16[4,128,768]{2,1,0:T(8,128)(2,1)S(1)}, u32[]{:S(2)}, u32[]{:S(2)}) async-start(bf16[4,128,768]{2,1,0:T(8,128)(2,1)} %bitcast.70), calls=%async_computation.5 | async-start | bytes 1572864 | tf_op jit(solution)/shard_map/all_to_all | solution.py:46
  412.9 8.4 %all-to-all-start.6 = ((f32[4,1,128]{2,1,0:T(1,128)}), f32[4,1,128]{2,1,0:T(1,128)S(1)}, u32[]{:S(2)}, u32[]{:S(2)}) async-start(f32[4,1,128]{2,1,0:T(1,128)} %broadcast_in_dim.28), calls=%async_computation.6 | async-start | bytes 4096 | tf_op jit(solution)/shard_map/all_to_all | solution.py:17
Sparse Core Ops, SparseCore 0:
  10.5 84.6 all-gather.5
  97.8 80.3 all-gather.7
  180.8 80.0 all-gather.9
  279.1 50.9 reduce-scatter.8
  332.5 56.0 reduce-scatter.4
  391.1 39.1 reduce-scatter.10
  432.8 38.2 reduce-scatter.6
where the time goes:
time: 481 us; the launch traced here: 480 us
  waiting for transfers between devices  322 us (67%)
  starting transfers between devices  37.8 us (8%)
  matrix products  32.2 us (7%)
  blocking collectives  28.8 us (6%)
  other arithmetic  23.3 us (5%)
  local copies, waits for them, and re-layouts  20.8 us (4%)
  between operations  14.5 us (3%)
    all_gather x3, waiting for transfers between devices, layer_rows(): return lax.all_gather(weight, DP, axis=0, tiled=True)  149 us
    reduce_scatter x4, waiting for transfers between devices, summed_rows(): shard = lax.psum_scatter(shard, axis, scatter_dimension=dim, tiled=True)  97 us
    all_to_all x2, waiting for transfers between devices, summed_on_arrival(): lax.all_to_all(cut_along(shard, dim, length), axis, 0, 0, tiled=True)  32.9 us
    all_to_all x3, waiting for transfers between devices, copy_for_each(): lax.all_to_all(jnp.broadcast_to(shard[None], (length, *shard.shape)), axi...  29.9 us
    all_to_all x2, blocking collectives, copy_for_each(): lax.all_to_all(jnp.broadcast_to(shard[None], (length, *shard.shape)), axi...  28.8 us
    all_to_all x3, starting transfers between devices, copy_for_each(): lax.all_to_all(jnp.broadcast_to(shard[None], (length, *shard.shape)), axi...  12 us
    all_to_all x1, waiting for transfers between devices, shards(): lax.all_to_all(outgoing, DP, split_axis=0, concat_axis=0, tiled=True)  11.1 us
    dot_general x2, matrix products, weight_sum(): lax.dot_general(left, right, (((0,), (0,)), ((), ())), preferred_element_...  10.3 us
  transfers between devices with their start and end apart: 15, of which 13 were waited for; matrix products, arithmetic and copies ran while one was open for 13% of the time, Pallas kernels for 0%

commit v1 on v0

--- a/solution.py
+++ b/solution.py
@@ -10,6 +10,18 @@
 DP = ("dp_0", "dp_1")
 epsilon = 1e-06
 levels = 1000.0
+
+
+def series_all_note(dimension_no, here_x, chip_axis):
+    return jnp.concatenate(
+        lax.all_to_all(
+            jnp.stack([here_x for _ in range(lax.axis_size(chip_axis))], axis=0),
+            axis_name=chip_axis,
+            split_axis=0,
+            concat_axis=0,
+        ),
+        axis=dimension_no,
+    )
 
 
 def copy_for_each(shard, axis):
@@ -78,7 +90,7 @@
 
 
 def layer_rows(weight):
-    return lax.all_gather(weight, DP, axis=0, tiled=True)
+    return series_all_note(0, weight, DP)
 
 
 def weight_sum(left, right):

time: 481 us -> 671 us (1.40)
  waiting for transfers between devices: 322 us -> 436 us
  starting transfers between devices: 37.8 us -> 69.9 us
  blocking collectives: 28.8 us -> 56 us
  local copies, waits for them, and re-layouts: 20.8 us -> 34 us
    all_to_all x0 -> x3, waiting for transfers between devices: none -> 290 us  [series_all_note(): lax.all_to_all(jnp.stack([here_x for _ in range(lax.axis_size(chip_axis))...]
    all_gather x3 -> x0, waiting for transfers between devices: 149 us -> none  [layer_rows(): return lax.all_gather(weight, DP, axis=0, tiled=True)]
    all_to_all x0 -> x3, starting transfers between devices: none -> 34.4 us  [series_all_note(): lax.all_to_all(jnp.stack([here_x for _ in range(lax.axis_size(chip_axis))...]
    all_to_all x2 -> x3, blocking collectives: 28.8 us -> 56 us  [copy_for_each(): lax.all_to_all(jnp.broadcast_to(shard[None], (length, *shard.shape)), axi...]
    all_to_all x3 -> x2, waiting for transfers between devices: 29.9 us -> 5.92 us  [copy_for_each(): lax.all_to_all(jnp.broadcast_to(shard[None], (length, *shard.shape)), axi...]
    reduce_scatter x4, waiting for transfers between devices: 97 us -> 84.2 us  [summed_rows(): shard = lax.psum_scatter(shard, axis, scatter_dimension=dim, tiled=True)]
    all_to_all x1, waiting for transfers between devices: 0.01 us -> 10.6 us  [shards(): lax.all_to_all(gap, DP, split_axis=0, concat_axis=0, tiled=True)]
    another operation x0 -> x3, local copies, waits for them, and re-layouts: none -> 9.06 us  [series_all_note(): jnp.stack([here_x for _ in range(lax.axis_size(chip_axis))], axis=0)]
  transfers between devices with their start and end apart: 15 -> 14, of which waited for: 13 -> 13; matrix products, arithmetic and copies ran while one was open for 13% -> 9% of each run, Pallas kernels for 0% -> 0%
where the time goes in v1:
time: 671 us; the launch traced here: 670 us
  waiting for transfers between devices  436 us (65%)
  starting transfers between devices  69.9 us (10%)
  blocking collectives  56 us (8%)
  local copies, waits for them, and re-layouts  34 us (5%)
  other arithmetic  29.9 us (4%)
  matrix products  29.9 us (4%)
  between operations  14.3 us (2%)
    all_to_all x3, waiting for transfers between devices, series_all_note(): lax.all_to_all(jnp.stack([here_x for _ in range(lax.axis_size(chip_axis))...  290 us
    reduce_scatter x4, waiting for transfers between devices, summed_rows(): shard = lax.psum_scatter(shard, axis, scatter_dimension=dim, tiled=True)  84.2 us
    all_to_all x3, blocking collectives, copy_for_each(): lax.all_to_all(jnp.broadcast_to(shard[None], (length, *shard.shape)), axi...  56 us
    all_to_all x3, starting transfers between devices, series_all_note(): lax.all_to_all(jnp.stack([here_x for _ in range(lax.axis_size(chip_axis))...  34.4 us
    all_to_all x2, waiting for transfers between devices, summed_on_arrival(): lax.all_to_all(cut_along(shard, dim, length), axis, 0, 0, tiled=True)  32.5 us
  transfers between devices with their start and end apart: 14, of which 13 were waited for; matrix products, arithmetic and copies ran while one was open for 9% of the time, Pallas kernels for 0%

profile of v1, /device:TPU:2, one launch (start us, length us, event | category | flops | bytes accessed | tf_op | source)
XLA Modules:
  0.0 670.0 jit_solution(9840461869124121993)
XLA Ops:
  8.1 16.6 %all_to_all.62 = bf16[4,128,768]{2,1,0:T(8,128)(2,1)S(1)} all-to-all(bf16[4,128,768]{2,1,0:T(8,128)(2,1)S(1)} %broadcast_in_dim.25), channel_id=1, replica_groups=mesh['role'=2,'dp_0'=4,'dp_1'=8,'mp'=4] {'mp'}, dimensions={0} | all-to-all | bytes 1572864 | tf_op jit(solution)/shard_map/all_to_all | solution.py:29
  24.7 3.6 stack.6
  28.3 11.8 %all-to-all-start.1 = ((bf16[32,96,768]{2,1,0:T(8,128)(2,1)}), bf16[32,96,768]{2,1,0:T(8,128)(2,1)}, u32[]{:S(2)}, u32[]{:S(2)}) async-start(bf16[32,96,768]{2,1,0:T(8,128)(2,1)} %stack.6), calls=%async_computation.1 | async-start | bytes 9437184 | tf_op jit(solution)/shard_map/all_to_all | solution.py:17
  43.2 98.5 %all-to-all-done.1 = bf16[32,96,768]{2,1,0:T(8,128)(2,1)} async-done(((bf16[32,96,768]{2,1,0:T(8,128)(2,1)}), bf16[32,96,768]{2,1,0:T(8,128)(2,1)}, u32[]{:S(2)}, u32[]{:S(2)}) %all-to-all-start.1) | async-done | bytes 4718624 | tf_op jit(solution)/shard_map/all_to_all | solution.py:17
  141.7 3.2 fusion.11
  146.4 10.8 %all-to-all-start.2 = ((bf16[32,8,768]{2,1,0:T(8,128)(2,1)}), bf16[32,8,768]{2,1,0:T(8,128)(2,1)S(1)}, u32[]{:S(2)}, u32[]{:S(2)}) async-start(bf16[32,8,768]{2,1,0:T(8,128)(2,1)} %reshape.184), calls=%async_computation.2 | async-start | bytes 786432 | tf_op jit(solution)/shard_map/all_to_all | solution.py:156
  157.4 12.9 %all-to-all-done.2 = bf16[32,8,768]{2,1,0:T(8,128)(2,1)S(1)} async-done(((bf16[32,8,768]{2,1,0:T(8,128)(2,1)}), bf16[32,8,768]{2,1,0:T(8,128)(2,1)S(1)}, u32[]{:S(2)}, u32[]{:S(2)}) %all-to-all-start.2) | async-done | bytes 393248 | tf_op jit(solution)/shard_map/all_to_all | solution.py:156
  171.3 19.9 %all_to_all.63 = bf16[4,256,768]{2,1,0:T(8,128)(2,1)S(1)} all-to-all(bf16[4,256,768]{2,1,0:T(8,128)(2,1)S(1)} %broadcast_in_dim.26), channel_id=1, replica_groups=mesh['role'=2,'dp_0'=4,'dp_1'=8,'mp'=4] {'mp'}, dimensions={0} | all-to-all | bytes 3145728 | tf_op jit(solution)/shard_map/all_to_all | solution.py:29
  191.2 2.8 stack.7
  194.0 9.4 %all-to-all-start.4 = ((bf16[32,96,768]{2,1,0:T(8,128)(2,1)}), bf16[32,96,768]{2,1,0:T(8,128)(2,1)}, u32[]{:S(2)}, u32[]{:S(2)}) async-start(bf16[32,96,768]{2,1,0:T(8,128)(2,1)} %stack.7), calls=%async_computation.4 | async-start | bytes 9437184 | tf_op jit(solution)/shard_map/all_to_all | solution.py:17
  206.9 1.9 multiply_convert_fusion.3
  208.8 97.9 %all-to-all-done.4 = bf16[32,96,768]{2,1,0:T(8,128)(2,1)} async-done(((bf16[32,96,768]{2,1,0:T(8,128)(2,1)}), bf16[32,96,768]{2,1,0:T(8,128)(2,1)}, u32[]{:S(2)}, u32[]{:S(2)}) %all-to-all-start.4) | async-done | bytes 4718624 | tf_op jit(solution)/shard_map/all_to_all | solution.py:17
  306.8 3.8 fusion.9
  310.7 19.5 %all_to_all.64 = bf16[4,256,768]{2,1,0:T(8,128)(2,1)} all-to-all(bf16[4,256,768]{2,1,0:T(8,128)(2,1)S(1)} %broadcast_in_dim.27), channel_id=1, replica_groups=mesh['role'=2,'dp_0'=4,'dp_1'=8,'mp'=4] {'mp'}, dimensions={0} | all-to-all | bytes 3145728 | tf_op jit(solution)/shard_map/all_to_all | solution.py:29
  330.3 2.7 stack.8
  333.0 13.2 %all-to-all-start.6 = ((bf16[32,96,768]{2,1,0:T(8,128)(2,1)}), bf16[32,96,768]{2,1,0:T(8,128)(2,1)}, u32[]{:S(2)}, u32[]{:S(2)}) async-start(bf16[32,96,768]{2,1,0:T(8,128)(2,1)} %stack.8), calls=%async_computation.6 | async-start | bytes 9437184 | tf_op jit(solution)/shard_map/all_to_all | solution.py:17
  348.2 1.7 copy.54
  349.9 1.9 convert_element_type.184
  352.8 2.1 multiply_convert_fusion.2
  354.9 93.4 %all-to-all-done.6 = bf16[32,96,768]{2,1,0:T(8,128)(2,1)} async-done(((bf16[32,96,768]{2,1,0:T(8,128)(2,1)}), bf16[32,96,768]{2,1,0:T(8,128)(2,1)}, u32[]{:S(2)}, u32[]{:S(2)}) %all-to-all-start.6) | async-done | bytes 4718624 | tf_op jit(solution)/shard_map/all_to_all | solution.py:17
  448.3 4.3 fusion.10
  452.7 3.6 copy.64
  456.3 5.7 fusion.12
  462.1 1.4 fusion.20
  463.9 4.2 convolution_convert_fusion
  468.1 3.8 convolution_convert_fusion.2
  473.2 3.6 all-to-all-start.10
  476.8 21.6 %all-to-all-done.10 = bf16[4,256,768]{2,1,0:T(8,128)(2,1)S(1)} async-done(((bf16[4,256,768]{2,1,0:T(8,128)(2,1)}), bf16[4,256,768]{2,1,0:T(8,128)(2,1)S(1)}, u32[]{:S(2)}, u32[]{:S(2)}) %all-to-all-start.10) | async-done | bytes 1572896 | tf_op jit(solution)/shard_map/all_to_all | solution.py:58
  498.6 2.9 multiply_reduce_fusion.3
  502.1 3.2 all-to-all-start.11
  505.4 2.0 convert_element_type.179
  507.5 2.4 copy.63
  511.9 6.0 convolution_convert_fusion.1
  518.0 2.9 reduce-scatter.9.cloned.1.call-done
  520.9 10.1 %all-to-all-start.7 = ((bf16[32,8,768]{2,1,0:T(8,128)(2,1)}), bf16[32,8,768]{2,1,0:T(8,128)(2,1)S(1)}, u32[]{:S(2)}, u32[]{:S(2)}) async-start(bf16[32,8,768]{2,1,0:T(8,128)(2,1)} %get-tuple-element.24), calls=%async_computation.7 | async-start | bytes 786432 | tf_op jit(solution)/shard_map/all_to_all | solution.py:190
  531.9 1.7 copy.56
  533.6 10.6 %all-to-all-done.7 = bf16[32,8,768]{2,1,0:T(8,128)(2,1)S(1)} async-done(((bf16[32,8,768]{2,1,0:T(8,128)(2,1)}), bf16[32,8,768]{2,1,0:T(8,128)(2,1)S(1)}, u32[]{:S(2)}, u32[]{:S(2)}) %all-to-all-start.7) | async-done | bytes 393248 | tf_op jit(solution)/shard_map/all_to_all | solution.py:190
  544.5 35.1 %reduce-scatter.5.cloned.1.call-done = bf16[768,768]{1,0:T(8,128)(2,1)} async-done(((bf16[3072,768]{1,0:T(8,128)(2,1)}), bf16[768,768]{1,0:T(8,128)(2,1)}) %reduce-scatter.5.cloned.1.call-update) | async-done | bytes 1179664 | tf_op jit(solution)/shard_map/reduce_scatter | solution.py:47
  580.1 4.1 convolution_convert_fusion.3
  585.1 4.3 all-to-all-start.8
  589.4 1.4 broadcast_multiply_fusion.1
  590.7 10.9 %all-to-all-done.8 = bf16[4,128,768]{2,1,0:T(8,128)(2,1)S(1)} async-done(((bf16[4,128,768]{2,1,0:T(8,128)(2,1)}), bf16[4,128,768]{2,1,0:T(8,128)(2,1)S(1)}, u32[]{:S(2)}, u32[]{:S(2)}) %all-to-all-start.8) | async-done | bytes 786464 | tf_op jit(solution)/shard_map/all_to_all | solution.py:58
  603.6 3.2 all-to-all-start.9
  606.9 5.2 all-to-all-done.9
  614.0 7.5 %reduce-scatter.11.cloned.1.call-done = bf16[96,768]{1,0:T(8,128)(2,1)} async-done(((bf16[768,768]{1,0:T(8,128)(2,1)}), bf16[96,768]{1,0:T(8,128)(2,1)}) %reduce-scatter.11.cloned.1.call-update) | async-done | bytes 147472 | tf_op jit(solution)/shard_map/reduce_scatter | solution.py:47
  621.5 1.6 bitcast_convert_fusion
  623.1 38.7 %reduce-scatter.7.cloned.1.call-done = bf16[96,768]{1,0:T(8,128)(2,1)} async-done(((bf16[768,768]{1,0:T(8,128)(2,1)}), bf16[96,768]{1,0:T(8,128)(2,1)}) %reduce-scatter.7.cloned.1.call-update) | async-done | bytes 147472 | tf_op jit(solution)/shard_map/reduce_scatter | solution.py:47
  661.8 1.6 bitcast_convert_fusion.1
  (125 shorter events, 24.5 us)
Async XLA Ops:
  28.3 11.8 %copy-start.16 = (f32[3072]{0:T(1024)S(1)}, f32[3072]{0:T(1024)}, u32[]{:S(2)}) copy-start(f32[3072]{0:T(1024)} %param.10) | copy-start | bytes 36868
  28.3 113.4 %all-to-all-start.1 = ((bf16[32,96,768]{2,1,0:T(8,128)(2,1)}), bf16[32,96,768]{2,1,0:T(8,128)(2,1)}, u32[]{:S(2)}, u32[]{:S(2)}) async-start(bf16[32,96,768]{2,1,0:T(8,128)(2,1)} %stack.6), calls=%async_computation.1 | async-start | bytes 9437184 | tf_op jit(solution)/shard_map/all_to_all | solution.py:17
  40.1 101.6 %copy-start.7 = (bf16[128,768]{1,0:T(8,128)(2,1)S(1)}, bf16[128,768]{1,0:T(8,128)(2,1)}, u32[]{:S(2)}) copy-start(bf16[128,768]{1,0:T(8,128)(2,1)} %param.9) | copy-start | bytes 589828
  41.9 103.2 %copy-start.23 = (s32[32]{0:T(128)}, s32[32]{0:T(128)S(1)}, u32[]{:S(2)}) copy-start(s32[32]{0:T(128)S(1)} %multiply_add_fusion.1) | copy-start | bytes 388
  42.3 102.7 %copy-start = (bf16[4,128,768]{1,2,0:T(8,128)(2,1)}, bf16[4,128,768]{1,2,0:T(8,128)(2,1)S(1)}, u32[]{:S(2)}) copy-start(bf16[4,128,768]{1,2,0:T(8,128)(2,1)S(1)} %copy.52) | copy-start | bytes 2359300
  42.7 99.0 %copy-start.25 = (f32[128]{0:T(128)}, f32[128]{0:T(128)S(1)}, u32[]{:S(2)}) copy-start(f32[128]{0:T(128)S(1)} %add_rsqrt_fusion.2) | copy-start | bytes 1540
  141.7 15.4 %copy-start.30 = (s32[64]{0:T(128)S(1)}, s32[64]{0:T(128)}, u32[]{:S(2)}) copy-start(s32[64]{0:T(128)} %param.14) | copy-start | bytes 772
  141.7 28.5 %copy-start.4 = (bf16[256,768]{1,0:T(8,128)(2,1)S(1)}, bf16[256,768]{1,0:T(8,128)(2,1)}, u32[]{:S(2)}) copy-start(bf16[256,768]{1,0:T(8,128)(2,1)} %param.13) | copy-start | bytes 1179652
  146.4 23.9 %all-to-all-start.2 = ((bf16[32,8,768]{2,1,0:T(8,128)(2,1)}), bf16[32,8,768]{2,1,0:T(8,128)(2,1)S(1)}, u32[]{:S(2)}, u32[]{:S(2)}) async-start(bf16[32,8,768]{2,1,0:T(8,128)(2,1)} %reshape.184), calls=%async_computation.2 | async-start | bytes 786432 | tf_op jit(solution)/shard_map/all_to_all | solution.py:156
  157.4 33.8 %copy-start.17 = (f32[256]{0:T(256)}, f32[256]{0:T(256)S(1)}, u32[]{:S(2)}) copy-start(f32[256]{0:T(256)S(1)} %broadcast_subtract_fusion) | copy-start | bytes 3076
  157.4 33.8 %copy-start.11 = (bf16[1,96,768]{2,1,0:T(8,128)(2,1)S(1)}, bf16[1,96,768]{2,1,0:T(8,128)(2,1)}, u32[]{:S(2)}) copy-start(bf16[1,96,768]{2,1,0:T(8,128)(2,1)} %param.16) | copy-start | bytes 442372
  170.5 0.7 copy-start.6
  194.0 9.4 %copy-start.15 = (f32[1,2,3072]{2,1,0:T(2,128)S(1)}, f32[1,2,3072]{2,1,0:T(2,128)}, u32[]{:S(2)}) copy-start(f32[1,2,3072]{2,1,0:T(2,128)} %param.15) | copy-start | bytes 73732
  194.0 112.8 %all-to-all-start.4 = ((bf16[32,96,768]{2,1,0:T(8,128)(2,1)}), bf16[32,96,768]{2,1,0:T(8,128)(2,1)}, u32[]{:S(2)}, u32[]{:S(2)}) async-start(bf16[32,96,768]{2,1,0:T(8,128)(2,1)} %stack.7), calls=%async_computation.4 | async-start | bytes 9437184 | tf_op jit(solution)/shard_map/all_to_all | solution.py:17
  206.3 0.6 copy-start.28
  310.6 19.7 %copy-start.10 = (bf16[256,768]{1,0:T(8,128)(2,1)}, bf16[256,768]{1,0:T(8,128)(2,1)S(1)}, u32[]{:S(2)}) copy-start(bf16[256,768]{1,0:T(8,128)(2,1)S(1)} %fusion.9) | copy-start | bytes 1179652
  310.6 19.7 %copy-start.12 = (bf16[1,96,768]{2,1,0:T(8,128)(2,1)S(1)}, bf16[1,96,768]{2,1,0:T(8,128)(2,1)}, u32[]{:S(2)}) copy-start(bf16[1,96,768]{2,1,0:T(8,128)(2,1)} %param.17) | copy-start | bytes 442372
  333.0 13.4 %copy-start.14 = (f32[3072]{0:T(1024)S(1)}, f32[3072]{0:T(1024)}, u32[]{:S(2)}) copy-start(f32[3072]{0:T(1024)} %get-tuple-element.16) | copy-start | bytes 36868
  333.0 14.1 %copy-start.22 = (s32[1024,1]{0,1:T(1,128)S(1)}, s32[1024,1]{0,1:T(1,128)}, u32[]{:S(2)}) copy-start(s32[1024,1]{0,1:T(1,128)} %param.12) | copy-start | bytes 12292
  333.0 115.4 %all-to-all-start.6 = ((bf16[32,96,768]{2,1,0:T(8,128)(2,1)}), bf16[32,96,768]{2,1,0:T(8,128)(2,1)}, u32[]{:S(2)}, u32[]{:S(2)}) async-start(bf16[32,96,768]{2,1,0:T(8,128)(2,1)} %stack.8), calls=%async_computation.6 | async-start | bytes 9437184 | tf_op jit(solution)/shard_map/all_to_all | solution.py:17
  346.2 174.7 %reduce-scatter.9.cloned.1.call-start = ((), (), s32[]{:S(2)}) async-start(), calls=%async_computation.18 | async-start | bytes 5898240 | tf_op jit(solution)/shard_map/reduce_scatter | solution.py:47
  349.9 3.0 copy-start.13
  352.3 0.5 copy-start.19
  452.6 9.4 %collective-permute-start = (bf16[256,768]{1,0:T(8,128)(2,1)S(1)}, bf16[256,768]{1,0:T(8,128)(2,1)S(1)}, u32[]{:S(2)}, u32[]{:S(2)}) collective-permute-start(bf16[256,768]{1,0:T(8,128)(2,1)S(1)} %fusion.10), channel_id=1, source_target_pairs={{0,128},{128,0},{1,129},{129,1},{2,130},{130,2},{3,131},{131,3},{4... | collective-permute-start | bytes 1179656 | tf_op jit(solution)/shard_map/ppermute | solution.py:73
  452.7 3.6 copy-start.20
  456.3 5.7 copy-start.5
  456.3 5.7 copy-start.18
  456.3 5.8 copy-start.27
  462.0 1.8 copy-start.3
  463.5 4.6 copy-start.8
  473.2 25.2 %all-to-all-start.10 = ((bf16[4,256,768]{2,1,0:T(8,128)(2,1)}), bf16[4,256,768]{2,1,0:T(8,128)(2,1)S(1)}, u32[]{:S(2)}, u32[]{:S(2)}) async-start(bf16[4,256,768]{2,1,0:T(8,128)(2,1)} %bitcast.88), calls=%async_computation.10 | async-start | bytes 3145728 | tf_op jit(solution)/shard_map/all_to_all | solution.py:58
  502.1 8.5 %all-to-all-start.11 = ((f32[4,1,256]{2,1,0:T(1,128)}), f32[4,1,256]{2,1,0:T(1,128)S(1)}, u32[]{:S(2)}, u32[]{:S(2)}) async-start(f32[4,1,256]{2,1,0:T(1,128)} %broadcast_in_dim.30), calls=%async_computation.11 | async-start | bytes 8192 | tf_op jit(solution)/shard_map/all_to_all | solution.py:29
  505.4 74.2 %reduce-scatter.5.cloned.1.call-start = ((), (), s32[]{:S(2)}) async-start(), calls=%async_computation.16 | async-start | bytes 5898240 | tf_op jit(solution)/shard_map/reduce_scatter | solution.py:47
  507.5 4.5 copy-start.9
  507.5 4.5 copy-start.21
  507.5 4.5 copy-start.29
  517.9 13.9 %copy-start.1 = (bf16[4,128,768]{1,2,0:T(8,128)(2,1)S(1)}, bf16[4,128,768]{1,2,0:T(8,128)(2,1)}, u32[]{:S(2)}) copy-start(bf16[4,128,768]{1,2,0:T(8,128)(2,1)} %copy-done) | copy-start | bytes 2359300
  517.9 103.6 %reduce-scatter.11.cloned.1.call-start = ((), (), s32[]{:S(2)}) async-start(), calls=%async_computation.19 | async-start | bytes 1327104 | tf_op jit(solution)/shard_map/reduce_scatter | solution.py:47
  520.9 23.3 %all-to-all-start.7 = ((bf16[32,8,768]{2,1,0:T(8,128)(2,1)}), bf16[32,8,768]{2,1,0:T(8,128)(2,1)S(1)}, u32[]{:S(2)}, u32[]{:S(2)}) async-start(bf16[32,8,768]{2,1,0:T(8,128)(2,1)} %get-tuple-element.24), calls=%async_computation.7 | async-start | bytes 786432 | tf_op jit(solution)/shard_map/all_to_all | solution.py:190
  531.0 130.8 %reduce-scatter.7.cloned.1.call-start = ((), (), s32[]{:S(2)}) async-start(), calls=%async_computation.17 | async-start | bytes 1327104 | tf_op jit(solution)/shard_map/reduce_scatter | solution.py:47
  531.9 47.7 %copy-start.24 = (s32[32]{0:T(128)S(1)}, s32[32]{0:T(128)}, u32[]{:S(2)}) copy-start(s32[32]{0:T(128)} %copy-done.23) | copy-start | bytes 388
  580.0 9.3 %copy-start.2 = (f32[128,3072]{1,0:T(8,128)S(1)}, f32[128,3072]{1,0:T(8,128)}, u32[]{:S(2)}) copy-start(f32[128,3072]{1,0:T(8,128)} %copy.56) | copy-start | bytes 4718596
  580.0 9.3 %copy-start.26 = (f32[128]{0:T(128)S(1)}, f32[128]{0:T(128)}, u32[]{:S(2)}) copy-start(f32[128]{0:T(128)} %copy-done.25) | copy-start | bytes 1540
  585.1 16.6 %all-to-all-start.8 = ((bf16[4,128,768]{2,1,0:T(8,128)(2,1)}), bf16[4,128,768]{2,1,0:T(8,128)(2,1)S(1)}, u32[]{:S(2)}, u32[]{:S(2)}) async-start(bf16[4,128,768]{2,1,0:T(8,128)(2,1)} %bitcast.85), calls=%async_computation.8 | async-start | bytes 1572864 | tf_op jit(solution)/shard_map/all_to_all | solution.py:58
  603.6 8.4 %all-to-all-start.9 = ((f32[4,1,128]{2,1,0:T(1,128)}), f32[4,1,128]{2,1,0:T(1,128)S(1)}, u32[]{:S(2)}, u32[]{:S(2)}) async-start(f32[4,1,128]{2,1,0:T(1,128)} %broadcast_in_dim.28), calls=%async_computation.9 | async-start | bytes 4096 | tf_op jit(solution)/shard_map/all_to_all | solution.py:29
Sparse Core Ops, SparseCore 0:
  468.2 52.6 reduce-scatter.8
  523.4 56.1 reduce-scatter.4
  582.2 39.2 reduce-scatter.10
  623.9 37.8 reduce-scatter.6
